TPU v7x, 32 devices: a whole 2x2x4 slice. The times are simulated.
32 devices in a mesh: grp: 4 (over y, x), lm: 8 (over z, core).
Axes of the slice: x: 2, y: 2, z: 4, core: 2. Of those that a mesh axis runs over, the one named last changes fastest.
Arguments:
- embeddings: bfloat16 [8192, 512], P(('grp', 'lm')), may hold values from -14 to 14
- landmarks: bfloat16 [16384, 512], P('lm'), may hold values from -14 to 14
- start_vectors: float32 [8192, 128], P(('grp', 'lm')), may hold values from -10 to 10
- row_weight: float32 [8192], P(('grp', 'lm')), may hold values from 0.1 to 9
- spread: float32 [1], replicated, may hold values from 11.313708 to 33.941124
Outputs:
- subspace: float32 [8192, 128], P(('grp', 'lm'))
All inputs are finite; a program needn't handle non-finite values.
Results may differ from a plain program's by a relative error of at most 0.019.
Values may be sent and summed in bfloat16 or wider, within the bound.
A program may use at most 128 MiB of HBM per device.

v0:
```python
import jax
import jax.numpy as jnp
from jax import lax
from jax.sharding import PartitionSpec as P

ITERS = 2


def unit_rows(values):
    values = values.astype(jnp.float32)
    scale = lax.rsqrt(jnp.sum(values * values, axis=1, keepdims=True) + 1e-06)
    return (values * scale).astype(jnp.bfloat16)


def kernel_values(rows_unit, marks_unit, gamma):
    cosine = jnp.einsum("rd,ld->rl", rows_unit, marks_unit, preferred_element_type=jnp.float32)
    return jnp.exp(gamma * cosine)


def local(embeddings, landmarks, start_vectors, row_weight, spread):
    own_rows = embeddings.shape[0]
    marks = landmarks.shape[0]
    groups = lax.axis_size("grp")
    members = lax.axis_size("lm")
    total_rows = own_rows * groups * members
    group_rows = own_rows * members
    gamma = spread[0]
    rows_unit = unit_rows(embeddings)
    marks_unit = unit_rows(landmarks)
    sums = jnp.zeros((marks,), jnp.float32)
    weights = jnp.zeros((group_rows,), jnp.float32)
    part_rows = lax.all_gather(rows_unit, "lm", axis=0, tiled=True)
    part_weight = lax.all_gather(row_weight.astype(jnp.bfloat16), "lm", axis=0, tiled=True).astype(
        jnp.float32
    )
    values = kernel_values(part_rows, marks_unit, gamma)
    build_tile = values.astype(jnp.bfloat16)
    weights = lax.dynamic_update_slice_in_dim(weights, part_weight, jnp.int32(0), 0)
    sums = sums + jnp.sum(part_weight[:, None] * values, axis=0)
    mean_sum, weight_sum = lax.psum((sums, jnp.sum(weights)), "grp")
    means = mean_sum / weight_sum
    vectors = start_vectors
    weighted_full = row_weight[:, None] * vectors
    totals = lax.psum(jnp.sum(weighted_full, axis=0), ("grp", "lm"))
    group_weighted = lax.all_gather(weighted_full.astype(jnp.bfloat16), "lm", axis=0, tiled=True)
    for step in range(ITERS):
        side = (
            lax.psum(
                jnp.einsum(
                    "rl,rv->lv", build_tile, group_weighted, preferred_element_type=jnp.float32
                ),
                "grp",
            )
            - means[:, None] * totals[None, :]
        )
        side_b = side.astype(jnp.bfloat16)
        shift = jnp.dot(means, side_b.astype(jnp.float32), precision=lax.Precision.HIGHEST)
        partial_rows = weights[:, None] * (
            jnp.dot(build_tile, side_b, preferred_element_type=jnp.float32) - shift[None, :]
        )
        image = lax.psum(partial_rows, "lm")
        square, column = lax.psum(
            (jnp.sum(image * image, axis=0), jnp.sum(weights[:, None] * image, axis=0)), "grp"
        )
        scale = jnp.sqrt(square / total_rows + 1e-06)
        group_vectors = image / scale[None, :]
        totals = column / scale
        group_weighted = (weights[:, None] * group_vectors).astype(jnp.bfloat16)
        vectors = lax.dynamic_slice_in_dim(
            group_vectors, lax.axis_index("lm") * own_rows, own_rows, 0
        )
    return vectors


def solution(mesh):
    in_specs = (
        P(("grp", "lm"), None),
        P("lm", None),
        P(("grp", "lm"), None),
        P(("grp", "lm")),
        P(),
    )
    out_specs = P(("grp", "lm"), None)
    return jax.shard_map(local, mesh=mesh, in_specs=in_specs, out_specs=out_specs, check_vma=False)
```

profile of v0, /device:TPU:0, one launch (start us, length us, event | category | flops | bytes accessed | tf_op | source)
XLA Modules:
  0.0 337.8 jit_solution(3544346859675565320)
XLA Ops:
  6.5 0.0 all-gather.3.cloned.1.call-start
  6.5 1.1 fusion.8
  7.6 1.8 fusion.9
  9.4 0.0 all-gather.3.cloned.1.call-update
  9.4 0.0 all-reduce.7.cloned.1.call-start
  9.5 0.7 convert_element_type.35
  10.2 13.5 %all-gather = bf16[8,1,256]{2,1,0:T(2,128)(2,1)S(1)} all-gather(bf16[1,1,256]{2,1,0:T(2,128)(2,1)S(1)} %reshape.21), channel_id=1, replica_groups=mesh['grp'=4,'lm'=8] {'lm'}, dimensions={0}, use_global_device_ids=true | all-gather | bytes 4608 | tf_op jit(solution)/shard_map/all_gather | solution.py:33
  24.3 2.1 fusion.1
  26.4 1.0 multiply_reduce_fusion.4
  27.4 17.3 %all_gather.11 = bf16[2048,128]{1,0:T(8,128)(2,1)S(1)} all-gather(bf16[256,128]{1,0:T(8,128)(2,1)S(1)} %get-tuple-element.14), channel_id=1, replica_groups=mesh['grp'=4,'lm'=8] {'lm'}, dimensions={0}, use_global_device_ids=true | all-gather | bytes 589824 | tf_op jit(solution)/shard_map/all_gather | solution.py:45
  44.7 1.0 all-gather.3.cloned.1.call-done
  45.7 7.8 %multiply_reduce_fusion = (f32[2048]{0:T(1024)S(1)}, bf16[2048,2048]{1,0:T(8,128)(2,1)S(1)}) fusion(f32[2048]{0:T(1024)S(1)} %bitcast.19, f32[]{:T(128)} %bitcast.16, bf16[2048,512]{1,0:T(8,128)(2,1)} %all-gather.3.cloned.1.call-done, bf16[2048,512]{1,0:T(8,128)(2,1)} %param.6, f32[2048]{0:T(1024)S(1)} %add_rsqrt_fusion), kind=kOutput, calls=%fused_computation | convolution fusion | flops 4314888192 | bytes 12607492 | tf_op jit(solution)/shard_map/rd,ld->rl/dot_general | solution.py:16
  53.5 0.0 copy-start
  53.5 3.2 copy-done
  56.7 3.4 %fusion.14 = f32[2048,128]{1,0:T(8,128)} fusion(bf16[2048,2048]{1,0:T(8,128)(2,1)S(1)} %get-tuple-element.12, bf16[2048,128]{1,0:T(8,128)(2,1)S(1)} %all_gather.11), kind=kOutput, calls=%fused_computation.38 | convolution fusion | flops 1073741824 | bytes 9961472 | tf_op jit(solution)/shard_map/rl,rv->lv/dot_general | solution.py:49
  60.2 0.0 all-reduce.7.cloned.1.call-update
  60.2 0.0 all-reduce.9.cloned.1.call-start
  60.2 40.3 %psum.73 = f32[128]{0:T(128)S(1)} all-reduce(f32[128]{0:T(128)S(1)} %get-tuple-element.13), channel_id=1, replica_groups=mesh['grp'=4,'lm'=8] {'grp','lm'}, use_global_device_ids=true, to_apply=%region_8.0 | all-reduce | flops 128 | bytes 1024 | tf_op jit(solution)/shard_map/psum | solution.py:44
  100.5 0.6 convert_reduce_fusion
  101.1 11.7 %all-reduce.1 = (f32[2048]{0:T(1024)S(1)}, f32[]{:T(128)}) all-reduce(f32[2048]{0:T(1024)S(1)} %get-tuple-element.11, f32[]{:T(128)} %convert_reduce_fusion), channel_id=1, replica_groups=mesh['grp'=4,'lm'=8] {'grp'}, use_global_device_ids=true, to_apply=%region_4.0 | all-reduce | flops 2049 | bytes 16392 | tf_op jit(solution)/shard_map/psum | solution.py:40
  112.8 0.6 broadcast_divide_fusion
  113.5 0.0 all-reduce.7.cloned.1.call-done
  113.5 1.8 convolution_bitcast_fusion.1
  115.3 7.1 %fusion.4 = f32[2048,128]{1,0:T(8,128)} fusion(bf16[2048,2048]{1,0:T(8,128)(2,1)} %copy-done, f32[128]{0:T(128)S(1)} %convolution_bitcast_fusion.1, f32[2048]{0:T(1024)S(1)} %bitcast.20, f32[2048,128]{1,0:T(8,128)} %all-reduce.7.cloned.1.call-done, f32[128]{0:T(128)S(1)} %psum.73, f32[2048]{0:T(1024)S(1)} %broadcast_divide_fusion), kind=kOutput, calls=%fused_computation.10 | convolution fusion | flops 1075052544 | bytes 10503168 | tf_op jit(solution)/shard_map/dot_general | solution.py:59
  122.4 0.0 all-reduce.9.cloned.1.call-update
  122.4 0.0 all-reduce.11.cloned.1.call-start
  122.5 58.7 %all-reduce.9.cloned.1.call-done = f32[2048,128]{1,0:T(8,128)} async-done(((f32[2048,128]{1,0:T(8,128)}), f32[2048,128]{1,0:T(8,128)}) %all-reduce.9.cloned.1.call-update) | async-done | bytes 1048592 | tf_op jit(solution)/shard_map/psum | solution.py:61
  181.1 1.6 multiply_reduce_fusion.2
  182.7 10.0 %all-reduce = (f32[128]{0:T(128)S(1)}, f32[128]{0:T(128)S(1)}) all-reduce(f32[128]{0:T(128)S(1)} %get-tuple-element.6, f32[128]{0:T(128)S(1)} %get-tuple-element.5), channel_id=1, replica_groups=mesh['grp'=4,'lm'=8] {'grp'}, use_global_device_ids=true, to_apply=%region_11.0 | all-reduce | flops 256 | bytes 2048 | tf_op jit(solution)/shard_map/psum | solution.py:62
  192.7 7.3 %fusion.10 = f32[2048,128]{1,0:T(8,128)} fusion(bf16[2048,2048]{1,0:T(8,128)(2,1)} %copy-done, f32[2048,128]{1,0:T(8,128)} %all-reduce.9.cloned.1.call-done, f32[128]{0:T(128)S(1)} %get-tuple-element.16, f32[2048]{0:T(1024)S(1)} %bitcast.22), kind=kOutput, calls=%fused_computation.25 | convolution fusion | flops 1074528256 | bytes 10494464 | tf_op jit(solution)/shard_map/rl,rv->lv/dot_general | solution.py:49
  200.0 0.0 all-reduce.11.cloned.1.call-update
  200.0 0.0 all-reduce.13.cloned.1.call-start
  200.1 49.9 %all-reduce.11.cloned.1.call-done = f32[2048,128]{1,0:T(8,128)} async-done(((f32[2048,128]{1,0:T(8,128)}), f32[2048,128]{1,0:T(8,128)}) %all-reduce.11.cloned.1.call-update) | async-done | bytes 1048592 | tf_op jit(solution)/shard_map/psum | solution.py:48
  250.0 1.8 convolution_bitcast_fusion
  251.8 7.1 %fusion.3 = f32[2048,128]{1,0:T(8,128)} fusion(bf16[2048,2048]{1,0:T(8,128)(2,1)} %copy-done, f32[128]{0:T(128)S(1)} %convolution_bitcast_fusion, f32[2048]{0:T(1024)S(1)} %bitcast.23, f32[2048,128]{1,0:T(8,128)} %all-reduce.11.cloned.1.call-done, f32[128]{0:T(128)S(1)} %get-tuple-element.15, f32[2048]{0:T(1024)S(1)} %broadcast_divide_fusion), kind=kOutput, calls=%fused_computation.8 | convolution fusion | flops 1075052544 | bytes 10503168 | tf_op jit(solution)/shard_map/dot_general | solution.py:59
  258.9 0.0 all-reduce.13.cloned.1.call-update
  258.9 59.5 %all-reduce.13.cloned.1.call-done = f32[2048,128]{1,0:T(8,128)} async-done(((f32[2048,128]{1,0:T(8,128)}), f32[2048,128]{1,0:T(8,128)}) %all-reduce.13.cloned.1.call-update) | async-done | bytes 1048592 | tf_op jit(solution)/shard_map/psum | solution.py:61
  318.4 1.5 multiply_reduce_fusion.1
  319.9 9.8 %psum.79 = f32[128]{0:T(128)S(1)} all-reduce(f32[128]{0:T(128)S(1)} %multiply_reduce_fusion.1), channel_id=1, replica_groups=mesh['grp'=4,'lm'=8] {'grp'}, use_global_device_ids=true, to_apply=%region_17.0 | all-reduce | flops 128 | bytes 1024 | tf_op jit(solution)/shard_map/psum | solution.py:62
  329.7 1.6 dynamic-slice_divide_fusion
  (6 shorter events, 0.1 us)
Async XLA Ops:
  6.5 39.1 %all-gather.3.cloned.1.call-start = ((), (), s32[]{:S(2)}) async-start(), calls=%async_computation | async-start | bytes 2359296 | tf_op jit(solution)/shard_map/all_gather | solution.py:32
  9.4 104.1 %all-reduce.7.cloned.1.call-start = ((), (), s32[]{:S(2)}) async-start(), calls=%async_computation.1 | async-start | bytes 2097152 | tf_op jit(solution)/shard_map/psum | solution.py:48
  53.5 3.2 copy-start
  60.2 120.9 %all-reduce.9.cloned.1.call-start = ((), (), s32[]{:S(2)}) async-start(), calls=%async_computation.2 | async-start | bytes 2097152 | tf_op jit(solution)/shard_map/psum | solution.py:61
  122.4 127.6 %all-reduce.11.cloned.1.call-start = ((), (), s32[]{:S(2)}) async-start(), calls=%async_computation.3 | async-start | bytes 2097152 | tf_op jit(solution)/shard_map/psum | solution.py:48
  200.0 118.3 %all-reduce.13.cloned.1.call-start = ((), (), s32[]{:S(2)}) async-start(), calls=%async_computation.4 | async-start | bytes 2097152 | tf_op jit(solution)/shard_map/psum | solution.py:61
Sparse Core Ops, SparseCore 0:
  9.6 36.0 all-gather.2
  60.3 52.8 all-reduce.6
  122.5 58.5 all-reduce.8
  200.2 49.8 all-reduce.10
  259.0 59.2 all-reduce.12
where the time goes:
time: 338 us
  waiting for transfers between devices  169 us (50%)
  blocking collectives  102 us (30%)
  matrix products  36.3 us (11%)
  between operations  13.9 us (4%)
  other arithmetic  12.6 us (4%)
    psum x2, waiting for transfers between devices, local(): image = lax.psum(partial_rows, 'lm')  118 us
    psum x2, waiting for transfers between devices, local(): lax.psum(jnp.einsum('rl,rv->lv', build_tile, group_weighted, preferred_el...  50 us
    psum x1, blocking collectives, local(): totals = lax.psum(jnp.sum(weighted_full, axis=0), ('grp', 'lm'))  40.3 us
    psum x2, blocking collectives, local(): lax.psum((jnp.sum(image * image, axis=0), jnp.sum(weights[:, None] * imag...  19.7 us
    all_gather x1, blocking collectives, local(): lax.all_gather(weighted_full.astype(jnp.bfloat16), 'lm', axis=0, tiled=True)  17.3 us
    dot_general x2, matrix products, local(): jnp.dot(build_tile, side_b, preferred_element_type=jnp.float32)  14.1 us
    all_gather x1, blocking collectives, local(): lax.all_gather(row_weight.astype(jnp.bfloat16), 'lm', axis=0, tiled=True)  13.5 us
    psum x1, blocking collectives, local(): mean_sum, weight_sum = lax.psum((sums, jnp.sum(weights)), 'grp')  11.7 us
  transfers between devices with their start and end apart: 5, of which 4 were waited for; matrix products, arithmetic and copies ran while one was open for 1% of the time, Pallas kernels for 0%

commit v1 on v0

v1 whole, which is shorter than its diff:
```python
import functools

import jax
import jax.numpy as jnp
from jax import lax
from jax.experimental import pallas as pl
from jax.experimental.pallas import tpu as pltpu
from jax.sharding import PartitionSpec as P

ITERS = 2
F32 = jnp.float32
BF16 = jnp.bfloat16
HIGHEST = lax.Precision.HIGHEST


def nt(a, b):
    return lax.dot_general(a, b, (((1,), (1,)), ((), ())), preferred_element_type=F32)


def nn(a, b):
    return jnp.dot(a, b, preferred_element_type=F32)


def tile(total, most):
    size = min(total, most)
    while total % size:
        size -= 8
    return size


def rows_at(index, size):
    return pl.ds(pl.multiple_of(index * size, size), size)


def kernel(
    groups, members, spread_ref, emb_ref, marks_ref, vec_ref, weight_ref, out_ref,
    marks_unit, kern, kern_t, unit, weighted, stats, side, means,
    side_out, side_in, side_stats_out, side_stats, side_b, shifts,
    image_out, pair_in, line_out, line_in, norms, group_norms,
    row_sems, stat_sems, grp_sems, img_sems, norm_sems,
):
    own, width = emb_ref.shape
    marks = marks_ref.shape[0]
    vecs = vec_ref.shape[1]
    part = marks // groups
    line = members // 2
    total_rows = own * groups * members
    me_g = lax.axis_index("grp")
    me_l = lax.axis_index("lm")
    z = me_l // 2
    c = me_l % 2
    sends = []

    def to(src, dst, send_sem, recv_sem, **device):
        copy = pltpu.make_async_remote_copy(
            src_ref=src, dst_ref=dst, send_sem=send_sem, recv_sem=recv_sem,
            device_id=device, device_id_type=pl.DeviceIdType.MESH,
        )
        copy.start()
        sends.append(copy)

    def arrived(ref, sem):
        pltpu.make_async_remote_copy(
            src_ref=ref, dst_ref=ref, send_sem=sem, recv_sem=sem,
            device_id={"lm": me_l}, device_id_type=pl.DeviceIdType.MESH,
        ).wait_recv()

    def mate():
        return z * 2 + 1 - c

    def along(k):
        return (z + k) % line * 2 + c

    def group(j):
        return (me_g + j) % groups

    order = sorted(range(1, line), key=lambda k: min(k, line - k))

    barrier = pltpu.get_barrier_semaphore()
    for k in range(1, members):
        pl.semaphore_signal(
            barrier, inc=1, device_id={"lm": (me_l + k) % members},
            device_id_type=pl.DeviceIdType.MESH,
        )
    for j in range(1, groups):
        pl.semaphore_signal(
            barrier, inc=1, device_id={"grp": group(j)}, device_id_type=pl.DeviceIdType.MESH
        )

    gamma = spread_ref[0]
    weight_row = weight_ref[...]
    weight = jnp.transpose(jnp.broadcast_to(weight_row, (128, own)))[:, :1]
    values = emb_ref[...].astype(F32)
    scale = lax.rsqrt(jnp.sum(values * values, axis=1, keepdims=True) + 1e-06)
    unit[0] = (values * scale).astype(BF16)
    full = weight * vec_ref[...]
    weighted[0, 0:own, :] = full.astype(BF16)
    stats[0, 0] = jnp.zeros(stats.shape[2:], F32)
    stats[0, 0, 0:1, 0:own] = weight_row
    stats[0, 0, 1:2, 0:vecs] = jnp.sum(full, axis=0, keepdims=True)

    pl.semaphore_wait(barrier, members - 1 + groups - 1)

    def chunk(step, slot):
        pieces = [
            (weighted.at[step, pl.ds(slot * own, own), :], row_sems.at[step, 1]),
            (stats.at[step, slot], row_sems.at[step, 2]),
        ]
        if step == 0:
            pieces.insert(0, (unit.at[slot], row_sems.at[step, 0]))
        return pieces

    def spread_chunk(step):
        for (src, sem), (dst, _) in zip(chunk(step, 0), chunk(step, line)):
            to(src, dst, sem.at[1, 0], sem.at[0, line], lm=mate())
        for k in order:
            back = line - k
            for (src, sem), (dst, _) in zip(chunk(step, 0), chunk(step, back)):
                to(src, dst, sem.at[1, k], sem.at[0, back], lm=along(k))

    def pass_on(step, k):
        for (src, sem), (dst, _) in zip(chunk(step, k), chunk(step, line + k)):
            to(src, dst, sem.at[1, line + k], sem.at[0, line + k], lm=mate())

    def await_chunk(step, slot):
        for ref, sem in chunk(step, slot):
            arrived(ref, sem.at[0, slot])

    spread_chunk(0)

    mark_tile = tile(part, 256)

    for j in range(groups):
        base = group(j) * part

        def unit_marks(i, carry, j=j, base=base):
            block = marks_ref[
                pl.ds(pl.multiple_of(base + i * mark_tile, mark_tile), mark_tile), :
            ].astype(F32)
            factor = lax.rsqrt(jnp.sum(block * block, axis=1, keepdims=True) + 1e-06)
            at = pl.ds(pl.multiple_of(j * part + i * mark_tile, mark_tile), mark_tile)
            marks_unit[at, :] = (block * factor).astype(BF16)
            return carry

        lax.fori_loop(0, part // mark_tile, unit_marks, 0)

    def build(slot):
        first = slot == 0
        here = pl.ds(slot * own, own)

        def visit(i, carry):
            at = rows_at(i, mark_tile)
            block = marks_unit[at, :]
            rows = unit[slot]
            tall = jnp.exp(gamma * nt(block, rows))
            tall_b = tall.astype(BF16)
            kern_t[at, here] = tall_b
            scaled = tall * stats[0, slot, 0:1, 0:own]
            fold = scaled[:, 0:128]
            for piece in range(1, own // 128):
                fold = fold + scaled[:, piece * 128 : (piece + 1) * 128]
            product = nn(tall_b, weighted[0, here, :])
            if first:
                means[at, :] = fold
                side[at, :] = product
            else:
                means[at, :] += fold
                side[at, :] += product
            kern[here, at] = jnp.exp(gamma * nt(rows, block)).astype(BF16)
            return carry

        lax.fori_loop(0, marks // mark_tile, visit, 0)

    build(0)
    await_chunk(0, line)
    build(line)
    for k in order:
        await_chunk(0, line - k)
        pass_on(0, line - k)
        build(line - k)
        await_chunk(0, 2 * line - k)
        build(2 * line - k)

    weight_sum = jnp.zeros((1, 1), F32)
    for slot in range(members):
        weight_sum = weight_sum + jnp.sum(stats[0, slot, 0:1, 0:own], axis=1, keepdims=True)

    def average(i, carry):
        at = rows_at(i, mark_tile)
        total = jnp.sum(means[at, :], axis=1, keepdims=True) / weight_sum
        means[at, :] = jnp.broadcast_to(total, (mark_tile, 128))
        return carry

    lax.fori_loop(0, marks // mark_tile, average, 0)

    line_tile = tile(own, 256)
    gaps = None
    mean_row = None
    image = None
    for step in range(ITERS):
        totals = stats[step, 0, 1:2, 0:vecs]
        squares = stats[step, 0, 2:3, 0:vecs]
        for slot in range(1, members):
            totals = totals + stats[step, slot, 1:2, 0:vecs]
            squares = squares + stats[step, slot, 2:3, 0:vecs]

        for j in [*range(1, groups), 0]:
            def centre(i, carry, j=j):
                at = pl.ds(pl.multiple_of(j * part + i * mark_tile, mark_tile), mark_tile)
                if step == 0:
                    product = side[at, :]
                else:
                    product = nn(kern_t[at, :], weighted[step])
                product = product - means[at, 0:1] * totals
                if j == 0:
                    side[at, :] = product
                else:
                    side_out[step, j, rows_at(i, mark_tile), :] = product.astype(BF16)
                return carry

            lax.fori_loop(0, part // mark_tile, centre, 0)
            side_stats_out[step, j] = jnp.zeros(side_stats_out.shape[2:], F32)
            if step == 0:
                side_stats_out[step, j, 0:1, 0:part] = jnp.transpose(
                    means[j * part : (j + 1) * part, :]
                )[0:1, :]
                side_stats_out[step, j, 1:2, 0:128] = jnp.broadcast_to(weight_sum, (1, 128))
            side_stats_out[step, j, 2:3, 0:vecs] = totals
            side_stats_out[step, j, 3:4, 0:vecs] = squares
            if j:
                back = groups - j
                to(
                    side_stats_out.at[step, j], side_stats.at[step, back],
                    grp_sems.at[step, 0, 1, j], grp_sems.at[step, 0, 0, back], grp=group(j),
                )
                to(
                    side_out.at[step, j], side_in.at[step, back],
                    grp_sems.at[step, 1, 1, j], grp_sems.at[step, 1, 0, back], grp=group(j),
                )
        said = [side_stats_out[step, 0]]
        for j in range(1, groups):
            arrived(side_stats.at[step, j], grp_sems.at[step, 0, 0, j])
            said.append(side_stats[step, j])
        if step == 0:
            all_weight = sum(s[1:2, 0:1] for s in said)
            mean_row = sum(s[0:1, 0:part] * (s[1:2, 0:1] / all_weight) for s in said)
            gaps = [s[0:1, 0:part] - mean_row for s in said]
            factor = None
        else:
            factor = 1.0 / jnp.sqrt(sum(s[3:4, 0:vecs] for s in said) / total_rows + 1e-06)
        pad = -groups % 8
        left = gaps + [jnp.zeros_like(gaps[0])] * pad
        right = [s[2:3, 0:vecs] for s in said]
        right = right + [jnp.zeros_like(right[0])] * pad
        correction = lax.dot_general(
            jnp.concatenate(left, axis=0), jnp.concatenate(right, axis=0),
            (((0,), (0,)), ((), ())), precision=HIGHEST, preferred_element_type=F32,
        )
        summed = side[0:part, :] + correction
        for j in range(1, groups):
            arrived(side_in.at[step, j], grp_sems.at[step, 1, 0, j])
            summed = summed + side_in[step, j].astype(F32)
        if factor is not None:
            summed = summed * factor
        rounded = summed.astype(BF16)
        side_b[step, 0:part, :] = rounded
        shift = jnp.dot(
            jnp.broadcast_to(mean_row, (8, part)), rounded.astype(F32),
            precision=HIGHEST, preferred_element_type=F32,
        )
        shifts[step, 0] = shift
        for j in range(1, groups):
            back = groups - j
            to(
                shifts.at[step, 0], shifts.at[step, back],
                grp_sems.at[step, 2, 1, j], grp_sems.at[step, 2, 0, back], grp=group(j),
            )
            to(
                side_b.at[step, pl.ds(0, part), :], side_b.at[step, pl.ds(back * part, part), :],
                grp_sems.at[step, 3, 1, j], grp_sems.at[step, 3, 0, back], grp=group(j),
            )
        for j in range(1, groups):
            arrived(shifts.at[step, j], grp_sems.at[step, 2, 0, j])
            shift = shift + shifts[step, j]
            arrived(
                side_b.at[step, pl.ds(j * part, part), :], grp_sems.at[step, 3, 0, j]
            )
        shift = shift[0:1, :]

        def product(slot):
            return nn(kern[slot * own : (slot + 1) * own, :], side_b[step]) - shift

        for k in [*order, 0]:
            image_out[step, k] = product(line + k).astype(BF16)
            to(
                image_out.at[step, k], pair_in.at[step, k],
                img_sems.at[step, 0, 1, k], img_sems.at[step, 0, 0, k], lm=mate(),
            )
        for k in order:
            mine = product(k)
            arrived(pair_in.at[step, k], img_sems.at[step, 0, 0, k])
            line_out[step, k] = (mine + pair_in[step, k].astype(F32)).astype(BF16)
            to(
                line_out.at[step, k], line_in.at[step, line - k],
                img_sems.at[step, 1, 1, k], img_sems.at[step, 1, 0, line - k], lm=along(k),
            )
        image = product(0)
        arrived(pair_in.at[step, 0], img_sems.at[step, 0, 0, 0])
        image = image + pair_in[step, 0].astype(F32)
        for k in order:
            arrived(line_in.at[step, line - k], img_sems.at[step, 1, 0, line - k])
            image = image + line_in[step, line - k].astype(F32)
        image = weight * image
        square = jnp.sum(image * image, axis=0, keepdims=True)
        if step < ITERS - 1:
            full = weight * image
            weighted[step + 1, 0:own, :] = full.astype(BF16)
            stats[step + 1, 0, 1:2, 0:vecs] = jnp.sum(full, axis=0, keepdims=True)
            stats[step + 1, 0, 2:3, 0:vecs] = square
            spread_chunk(step + 1)
            for k in order:
                await_chunk(step + 1, line - k)
                pass_on(step + 1, line - k)
            await_chunk(step + 1, line)
            for k in order:
                await_chunk(step + 1, 2 * line - k)

    norms[0] = jnp.broadcast_to(square, norms.shape[1:])
    for k in range(1, members):
        back = members - k
        to(
            norms.at[0], norms.at[back], norm_sems.at[1, k], norm_sems.at[0, back],
            lm=(me_l + k) % members,
        )
    for k in range(1, members):
        arrived(norms.at[k], norm_sems.at[0, k])
        square = square + norms[k, 0:1, :]
    group_norms[0] = jnp.broadcast_to(square, norms.shape[1:])
    for j in range(1, groups):
        back = groups - j
        to(
            group_norms.at[0], group_norms.at[back],
            norm_sems.at[1, members + j], norm_sems.at[0, members + back], grp=group(j),
        )
    for j in range(1, groups):
        arrived(group_norms.at[j], norm_sems.at[0, members + j])
        square = square + group_norms[j, 0:1, :]
    out_ref[...] = image / jnp.sqrt(square / total_rows + 1e-06)
    for copy in sends:
        copy.wait_send()


def local(groups, members, embeddings, landmarks, start_vectors, row_weight, spread):
    own, width = embeddings.shape
    marks = landmarks.shape[0]
    vecs = start_vectors.shape[1]
    rows = own * members
    part = marks // groups
    line = members // 2
    wide = max(own, vecs)
    span = max(part, vecs)
    vmem = pl.BlockSpec(memory_space=pltpu.VMEM)
    dma = pltpu.SemaphoreType.DMA
    return pl.pallas_call(
        functools.partial(kernel, groups, members),
        out_shape=jax.ShapeDtypeStruct((own, vecs), F32),
        in_specs=[pl.BlockSpec(memory_space=pltpu.SMEM), vmem, vmem, vmem, vmem],
        out_specs=vmem,
        scratch_shapes=[
            pltpu.VMEM((marks, width), BF16),
            pltpu.VMEM((rows, marks), BF16),
            pltpu.VMEM((marks, rows), BF16),
            pltpu.VMEM((members, own, width), BF16),
            pltpu.VMEM((ITERS, rows, vecs), BF16),
            pltpu.VMEM((ITERS, members, 8, wide), F32),
            pltpu.VMEM((marks, vecs), F32),
            pltpu.VMEM((marks, 128), F32),
            pltpu.VMEM((ITERS, groups, part, vecs), BF16),
            pltpu.VMEM((ITERS, groups, part, vecs), BF16),
            pltpu.VMEM((ITERS, groups, 8, span), F32),
            pltpu.VMEM((ITERS, groups, 8, span), F32),
            pltpu.VMEM((ITERS, marks, vecs), BF16),
            pltpu.VMEM((ITERS, groups, 8, vecs), F32),
            pltpu.VMEM((ITERS, line, own, vecs), BF16),
            pltpu.VMEM((ITERS, line, own, vecs), BF16),
            pltpu.VMEM((ITERS, line, own, vecs), BF16),
            pltpu.VMEM((ITERS, line, own, vecs), BF16),
            pltpu.VMEM((members, 8, vecs), F32),
            pltpu.VMEM((groups, 8, vecs), F32),
            dma((ITERS, 3, 2, members)),
            dma((1,)),
            dma((ITERS, 4, 2, groups)),
            dma((ITERS, 2, 2, line)),
            dma((2, members + groups)),
        ],
        compiler_params=pltpu.CompilerParams(
            collective_id=0, has_side_effects=True, vmem_limit_bytes=62 * 2**20
        ),
    )(spread, embeddings, landmarks, start_vectors, row_weight.reshape(1, own))


def solution(mesh):
    groups, members = mesh.shape["grp"], mesh.shape["lm"]
    in_specs = (
        P(("grp", "lm"), None),
        P("lm", None),
        P(("grp", "lm"), None),
        P(("grp", "lm")),
        P(),
    )
    return jax.shard_map(
        functools.partial(local, groups, members), mesh=mesh, in_specs=in_specs,
        out_specs=P(("grp", "lm"), None), check_vma=False,
    )
```

time: 338 us -> 119 us (0.35)
  waiting for transfers between devices: 169 us -> 0 us
  Pallas kernels: 0 us -> 116 us
  blocking collectives: 102 us -> 0 us
  matrix products: 36.3 us -> 0 us
  between operations: 13.9 us -> 0.66 us
  other arithmetic: 12.6 us -> 0 us
    psum x4 -> x0, waiting for transfers between devices: 168 us -> none  [the longest x2 118 us: local(): image = lax.psum(partial_rows, 'lm')]
    pallas_call x0 -> x1, Pallas kernels: none -> 116 us  [local(): pl.pallas_call(functools.partial(kernel, groups, members), out_shape=jax....]
    psum x4 -> x0, blocking collectives: 71.7 us -> none  [the longest x1 40.3 us: local(): totals = lax.psum(jnp.sum(weighted_full, axis=0), ('grp', 'lm'))]
    dot_general x7 -> x0, matrix products: 36.3 us -> none  [the longest x2 14.1 us: local(): jnp.dot(build_tile, side_b, preferred_element_type=jnp.float32)]
    all_gather x2 -> x0, blocking collectives: 30.8 us -> none  [the longest x1 17.3 us: local(): lax.all_gather(weighted_full.astype(jnp.bfloat16), 'lm', axis=0, tiled=True)]
    reduce_sum x6 -> x0, other arithmetic: 7.87 us -> none  [the longest x2 3.15 us: unit_rows(): scale = lax.rsqrt(jnp.sum(values * values, axis=1, keepdims=True) + 1e-06)]
  transfers between devices with their start and end apart: 5 -> 0, of which waited for: 4 -> 0; matrix products, arithmetic and copies ran while one was open for 1% -> 0% of each run, Pallas kernels for 0% -> 0%
where the time goes in v1:
time: 119 us; the launch traced here: 118 us
  Pallas kernels  116 us (97%)
  local copies, waits for them, and re-layouts  1.57 us (1%)
    pallas_call x1, Pallas kernels, local(): pl.pallas_call(functools.partial(kernel, groups, members), out_shape=jax....  116 us

profile of v1, /device:TPU:0, one launch (start us, length us, event | category | flops | bytes accessed | tf_op | source)
XLA Modules:
  0.0 118.4 jit_solution(6276987233887228583)
XLA Ops:
  0.7 116.2 %shard_map.55 = f32[256,128]{1,0:T(8,128)} custom-call(f32[1]{0:T(128)S(6)} %copy.7.spread_ref, bf16[256,512]{1,0:T(8,128)(2,1)} %emb_ref.1, bf16[2048,512]{1,0:T(8,128)(2,1)} %marks_ref.1, f32[256,128]{1,0:T(8,128)} %vec_ref.1, f32[1,256]{1,0:T(1,128)} %bitcast.1), custom_call_target="tpu_custom_call" | custom-call | tf_op jit(solution)/shard_map/pallas_call | solution.py:364
  116.9 1.6 %copy.8 = f32[256,128]{1,0:T(8,128)} copy(f32[256,128]{1,0:T(8,128)} %shard_map.55) | data formatting | bytes 262144

commit v2 on v1

--- a/solution.py
+++ b/solution.py
@@ -10,6 +10,7 @@
 ITERS = 2
 F32 = jnp.float32
 BF16 = jnp.bfloat16
+BUILD = 1024
 HIGHEST = lax.Precision.HIGHEST
 
 
@@ -34,10 +35,10 @@
 
 def kernel(
     groups, members, spread_ref, emb_ref, marks_ref, vec_ref, weight_ref, out_ref,
-    marks_unit, kern, kern_t, unit, weighted, stats, side, means,
+    marks_in, marks_unit, kern_t, unit, weighted, stats, side, means,
     side_out, side_in, side_stats_out, side_stats, side_b, shifts,
     image_out, pair_in, line_out, line_in, norms, group_norms,
-    row_sems, stat_sems, grp_sems, img_sems, norm_sems,
+    row_sems, stat_sems, grp_sems, img_sems, norm_sems, mark_sems, grown,
 ):
     own, width = emb_ref.shape
     marks = marks_ref.shape[0]
@@ -50,14 +51,18 @@
     z = me_l // 2
     c = me_l % 2
     sends = []
-
-    def to(src, dst, send_sem, recv_sem, **device):
+    half = own // 2
+
+    def to(src, dst, send_sem, recv_sem, when=None, **device):
         copy = pltpu.make_async_remote_copy(
             src_ref=src, dst_ref=dst, send_sem=send_sem, recv_sem=recv_sem,
             device_id=device, device_id_type=pl.DeviceIdType.MESH,
         )
-        copy.start()
-        sends.append(copy)
+        if when is None:
+            copy.start()
+        else:
+            pl.when(when)(copy.start)
+        sends.append((when, copy))
 
     def arrived(ref, sem):
         pltpu.make_async_remote_copy(
@@ -86,6 +91,14 @@
         pl.semaphore_signal(
             barrier, inc=1, device_id={"grp": group(j)}, device_id_type=pl.DeviceIdType.MESH
         )
+
+    mark_copies = []
+    for j in range(groups):
+        mark_copies.append(pltpu.make_async_copy(
+            marks_ref.at[pl.ds(pl.multiple_of(group(j) * part, part), part), :],
+            marks_in.at[pl.ds(j * part, part), :], mark_sems.at[j],
+        ))
+        mark_copies[j].start()
 
     gamma = spread_ref[0]
     weight_row = weight_ref[...]
@@ -93,12 +106,6 @@
     values = emb_ref[...].astype(F32)
     scale = lax.rsqrt(jnp.sum(values * values, axis=1, keepdims=True) + 1e-06)
     unit[0] = (values * scale).astype(BF16)
-    full = weight * vec_ref[...]
-    weighted[0, 0:own, :] = full.astype(BF16)
-    stats[0, 0] = jnp.zeros(stats.shape[2:], F32)
-    stats[0, 0, 0:1, 0:own] = weight_row
-    stats[0, 0, 1:2, 0:vecs] = jnp.sum(full, axis=0, keepdims=True)
-
     pl.semaphore_wait(barrier, members - 1 + groups - 1)
 
     def chunk(step, slot):
@@ -107,8 +114,54 @@
             (stats.at[step, slot], row_sems.at[step, 2]),
         ]
         if step == 0:
-            pieces.insert(0, (unit.at[slot], row_sems.at[step, 0]))
+            pieces = [
+                (unit.at[slot, pl.ds(0, half), :], row_sems.at[step, 0]),
+                (unit.at[slot, pl.ds(half, half), :], row_sems.at[step, 3]),
+            ] + pieces
         return pieces
+
+    def chunk_at(slot):
+        return [
+            (unit.at[slot, pl.ds(0, half), :], row_sems.at[0, 0]),
+            (unit.at[slot, pl.ds(half, half), :], row_sems.at[0, 3]),
+            (weighted.at[0, pl.ds(pl.multiple_of(slot * own, own), own), :], row_sems.at[0, 1]),
+            (stats.at[0, slot], row_sems.at[0, 2]),
+        ]
+
+    def send_own(low, high):
+        for right in (1, 0):
+            slot = line - 1 if right else 1
+            pieces = zip(chunk(0, 0)[low:high], chunk(0, slot)[low:high])
+            for (src, sem), (dst, _) in pieces:
+                to(
+                    src, dst, sem.at[1, right * line], sem.at[0, slot],
+                    when=z < line - 1 if right else z > 0,
+                    lm=(z + 1 if right else z - 1) * 2 + c,
+                )
+        for (src, sem), (dst, _) in zip(chunk(0, 0)[low:high], chunk(0, line)[low:high]):
+            to(src, dst, sem.at[2, 0], sem.at[0, line], lm=mate())
+
+    def next_slot(t):
+        both = jnp.minimum(z, line - 1 - z)
+        near = t < 2 * both
+        far = jnp.where(near, t // 2 + 1, t - both + 1)
+        left = jnp.where(near, t % 2, jnp.where(2 * z < line - 1, 1, 0)) == 0
+        return jnp.where(left, line - far, far), left
+
+    def relay(t):
+        slot, left = next_slot(t)
+        beyond = jnp.where(left, slot - 1, slot + 1)
+        more = jnp.where(left, z < line - 1, z > 0)
+        follow = jnp.where(more, beyond, slot)
+        for (src, sem), (dst, _) in zip(chunk_at(slot), chunk_at(follow)):
+            arrived(src, sem.at[0, slot])
+            to(
+                src, dst, sem.at[1, slot + jnp.where(left, line, 0)], sem.at[0, follow],
+                when=more, lm=jnp.where(left, z + 1, z - 1) % line * 2 + c,
+            )
+        for (src, sem), (dst, _) in zip(chunk_at(slot), chunk_at(line + slot)):
+            to(src, dst, sem.at[2, slot], sem.at[0, line + slot], lm=mate())
+        return slot
 
     def spread_chunk(step):
         for (src, sem), (dst, _) in zip(chunk(step, 0), chunk(step, line)):
@@ -126,33 +179,36 @@
         for ref, sem in chunk(step, slot):
             arrived(ref, sem.at[0, slot])
 
-    spread_chunk(0)
+    send_own(0, 2)
+    full = weight * vec_ref[...]
+    weighted[0, 0:own, :] = full.astype(BF16)
+    stats[0, 0] = jnp.zeros(stats.shape[2:], F32)
+    stats[0, 0, 0:1, 0:own] = weight_row
+    stats[0, 0, 1:2, 0:vecs] = jnp.sum(full, axis=0, keepdims=True)
+
+    send_own(2, 4)
 
     mark_tile = tile(part, 256)
 
+    def unit_marks(i, carry):
+        at = rows_at(i, mark_tile)
+        block = marks_in[at, :].astype(F32)
+        factor = lax.rsqrt(jnp.sum(block * block, axis=1, keepdims=True) + 1e-06)
+        marks_unit[at, :] = (block * factor).astype(BF16)
+        return carry
+
     for j in range(groups):
-        base = group(j) * part
-
-        def unit_marks(i, carry, j=j, base=base):
-            block = marks_ref[
-                pl.ds(pl.multiple_of(base + i * mark_tile, mark_tile), mark_tile), :
-            ].astype(F32)
-            factor = lax.rsqrt(jnp.sum(block * block, axis=1, keepdims=True) + 1e-06)
-            at = pl.ds(pl.multiple_of(j * part + i * mark_tile, mark_tile), mark_tile)
-            marks_unit[at, :] = (block * factor).astype(BF16)
-            return carry
-
-        lax.fori_loop(0, part // mark_tile, unit_marks, 0)
-
-    def build(slot):
-        first = slot == 0
-        here = pl.ds(slot * own, own)
+        mark_copies[j].wait()
+        lax.fori_loop(
+            j * part // mark_tile, (j + 1) * part // mark_tile, unit_marks, 0
+        )
+
+    def build(slot, first=False):
+        here = pl.ds(pl.multiple_of(slot * own, own), own)
 
         def visit(i, carry):
-            at = rows_at(i, mark_tile)
-            block = marks_unit[at, :]
-            rows = unit[slot]
-            tall = jnp.exp(gamma * nt(block, rows))
+            at = rows_at(i, build_tile)
+            tall = jnp.exp(gamma * nt(marks_unit[at, :], unit[slot]))
             tall_b = tall.astype(BF16)
             kern_t[at, here] = tall_b
             scaled = tall * stats[0, slot, 0:1, 0:own]
@@ -166,20 +222,20 @@
             else:
                 means[at, :] += fold
                 side[at, :] += product
-            kern[here, at] = jnp.exp(gamma * nt(rows, block)).astype(BF16)
             return carry
 
-        lax.fori_loop(0, marks // mark_tile, visit, 0)
-
-    build(0)
+        lax.fori_loop(0, marks // build_tile, visit, 0)
+
+    build_tile = tile(marks, BUILD)
+    build(0, True)
     await_chunk(0, line)
     build(line)
-    for k in order:
-        await_chunk(0, line - k)
-        pass_on(0, line - k)
-        build(line - k)
-        await_chunk(0, 2 * line - k)
-        build(2 * line - k)
+    for t in range(line - 1):
+        slot = relay(t)
+        build(slot)
+        for ref, sem in chunk_at(line + slot):
+            arrived(ref, sem.at[0, line + slot])
+        build(line + slot)
 
     weight_sum = jnp.zeros((1, 1), F32)
     for slot in range(members):
@@ -193,7 +249,18 @@
 
     lax.fori_loop(0, marks // mark_tile, average, 0)
 
-    line_tile = tile(own, 256)
+    def gather_term(step, slot):
+        def visit(i, carry):
+            at = rows_at(i, build_tile)
+            product = nn(
+                kern_t[at, slot * own : (slot + 1) * own],
+                weighted[step, slot * own : (slot + 1) * own, :],
+            )
+            side[at, :] = product if slot == 0 else side[at, :] + product
+            return carry
+
+        lax.fori_loop(0, marks // build_tile, visit, 0)
+
     gaps = None
     mean_row = None
     image = None
@@ -207,11 +274,7 @@
         for j in [*range(1, groups), 0]:
             def centre(i, carry, j=j):
                 at = pl.ds(pl.multiple_of(j * part + i * mark_tile, mark_tile), mark_tile)
-                if step == 0:
-                    product = side[at, :]
-                else:
-                    product = nn(kern_t[at, :], weighted[step])
-                product = product - means[at, 0:1] * totals
+                product = side[at, :] - means[at, 0:1] * totals
                 if j == 0:
                     side[at, :] = product
                 else:
@@ -263,7 +326,7 @@
         if factor is not None:
             summed = summed * factor
         rounded = summed.astype(BF16)
-        side_b[step, 0:part, :] = rounded
+        side_b[step, 0] = jnp.transpose(summed).astype(BF16)
         shift = jnp.dot(
             jnp.broadcast_to(mean_row, (8, part)), rounded.astype(F32),
             precision=HIGHEST, preferred_element_type=F32,
@@ -276,19 +339,29 @@
                 grp_sems.at[step, 2, 1, j], grp_sems.at[step, 2, 0, back], grp=group(j),
             )
             to(
-                side_b.at[step, pl.ds(0, part), :], side_b.at[step, pl.ds(back * part, part), :],
+                side_b.at[step, 0], side_b.at[step, back],
                 grp_sems.at[step, 3, 1, j], grp_sems.at[step, 3, 0, back], grp=group(j),
             )
-        for j in range(1, groups):
-            arrived(shifts.at[step, j], grp_sems.at[step, 2, 0, j])
-            shift = shift + shifts[step, j]
-            arrived(
-                side_b.at[step, pl.ds(j * part, part), :], grp_sems.at[step, 3, 0, j]
-            )
-        shift = shift[0:1, :]
+        def term(j, slot):
+            block = kern_t[j * part : (j + 1) * part, slot * own : (slot + 1) * own]
+            return nn(side_b[step, j], block)
+
+        for j in range(groups):
+            if j:
+                arrived(shifts.at[step, j], grp_sems.at[step, 2, 0, j])
+                shift = shift + shifts[step, j]
+                arrived(side_b.at[step, j], grp_sems.at[step, 3, 0, j])
+            if j < groups - 1:
+                for slot in range(members):
+                    if j == 0:
+                        grown[slot] = term(j, slot)
+                    else:
+                        grown[slot] += term(j, slot)
+        shift = jnp.transpose(jnp.broadcast_to(shift[0:1, :], (128, vecs)))[:, 0:1]
 
         def product(slot):
-            return nn(kern[slot * own : (slot + 1) * own, :], side_b[step]) - shift
+            last = term(groups - 1, slot) - shift
+            return last if groups == 1 else grown[slot] + last
 
         for k in [*order, 0]:
             image_out[step, k] = product(line + k).astype(BF16)
@@ -310,7 +383,7 @@
         for k in order:
             arrived(line_in.at[step, line - k], img_sems.at[step, 1, 0, line - k])
             image = image + line_in[step, line - k].astype(F32)
-        image = weight * image
+        image = weight * jnp.transpose(image)
         square = jnp.sum(image * image, axis=0, keepdims=True)
         if step < ITERS - 1:
             full = weight * image
@@ -318,12 +391,16 @@
             stats[step + 1, 0, 1:2, 0:vecs] = jnp.sum(full, axis=0, keepdims=True)
             stats[step + 1, 0, 2:3, 0:vecs] = square
             spread_chunk(step + 1)
+            gather_term(step + 1, 0)
+            await_chunk(step + 1, line)
+            gather_term(step + 1, line)
             for k in order:
                 await_chunk(step + 1, line - k)
                 pass_on(step + 1, line - k)
-            await_chunk(step + 1, line)
+                gather_term(step + 1, line - k)
             for k in order:
                 await_chunk(step + 1, 2 * line - k)
+                gather_term(step + 1, 2 * line - k)
 
     norms[0] = jnp.broadcast_to(square, norms.shape[1:])
     for k in range(1, members):
@@ -346,8 +423,11 @@
         arrived(group_norms.at[j], norm_sems.at[0, members + j])
         square = square + group_norms[j, 0:1, :]
     out_ref[...] = image / jnp.sqrt(square / total_rows + 1e-06)
-    for copy in sends:
-        copy.wait_send()
+    for when, copy in sends:
+        if when is None:
+            copy.wait_send()
+        else:
+            pl.when(when)(copy.wait_send)
 
 
 def local(groups, members, embeddings, landmarks, start_vectors, row_weight, spread):
@@ -364,11 +444,11 @@
     return pl.pallas_call(
         functools.partial(kernel, groups, members),
         out_shape=jax.ShapeDtypeStruct((own, vecs), F32),
-        in_specs=[pl.BlockSpec(memory_space=pltpu.SMEM), vmem, vmem, vmem, vmem],
+        in_specs=[pl.BlockSpec(memory_space=pltpu.SMEM), vmem, pl.BlockSpec(memory_space=pl.ANY), vmem, vmem],
         out_specs=vmem,
         scratch_shapes=[
             pltpu.VMEM((marks, width), BF16),
-            pltpu.VMEM((rows, marks), BF16),
+            pltpu.VMEM((marks, width), BF16),
             pltpu.VMEM((marks, rows), BF16),
             pltpu.VMEM((members, own, width), BF16),
             pltpu.VMEM((ITERS, rows, vecs), BF16),
@@ -379,19 +459,21 @@
             pltpu.VMEM((ITERS, groups, part, vecs), BF16),
             pltpu.VMEM((ITERS, groups, 8, span), F32),
             pltpu.VMEM((ITERS, groups, 8, span), F32),
-            pltpu.VMEM((ITERS, marks, vecs), BF16),
+            pltpu.VMEM((ITERS, groups, vecs, part), BF16),
             pltpu.VMEM((ITERS, groups, 8, vecs), F32),
-            pltpu.VMEM((ITERS, line, own, vecs), BF16),
-            pltpu.VMEM((ITERS, line, own, vecs), BF16),
-            pltpu.VMEM((ITERS, line, own, vecs), BF16),
-            pltpu.VMEM((ITERS, line, own, vecs), BF16),
+            pltpu.VMEM((ITERS, line, vecs, own), BF16),
+            pltpu.VMEM((ITERS, line, vecs, own), BF16),
+            pltpu.VMEM((ITERS, line, vecs, own), BF16),
+            pltpu.VMEM((ITERS, line, vecs, own), BF16),
             pltpu.VMEM((members, 8, vecs), F32),
             pltpu.VMEM((groups, 8, vecs), F32),
-            dma((ITERS, 3, 2, members)),
+            dma((ITERS, 4, 3, members)),
             dma((1,)),
             dma((ITERS, 4, 2, groups)),
             dma((ITERS, 2, 2, line)),
             dma((2, members + groups)),
+            dma((groups,)),
+            pltpu.VMEM((members, vecs, own), F32),
         ],
         compiler_params=pltpu.CompilerParams(
             collective_id=0, has_side_effects=True, vmem_limit_bytes=62 * 2**20

time: 119 us -> 113 us (0.950)
  Pallas kernels: 116 us -> 111 us
    pallas_call x1, Pallas kernels: 116 us -> 111 us  [local(): pl.pallas_call(functools.partial(kernel, groups, members), out_shape=jax....]
where the time goes in v2:
time: 113 us
  Pallas kernels  111 us (98%)
  local copies, waits for them, and re-layouts  1.57 us (1%)
    pallas_call x1, Pallas kernels, local(): pl.pallas_call(functools.partial(kernel, groups, members), out_shape=jax....  111 us

profile of v2, /device:TPU:0, one launch (start us, length us, event | category | flops | bytes accessed | tf_op | source)
XLA Modules:
  0.0 113.1 jit_solution(12165887524852097044)
XLA Ops:
  0.7 110.8 %shard_map.55 = f32[256,128]{1,0:T(8,128)} custom-call(f32[1]{0:T(128)S(6)} %copy.7.spread_ref, bf16[256,512]{1,0:T(8,128)(2,1)} %emb_ref.1, bf16[2048,512]{1,0:T(8,128)(2,1)} %marks_ref.1, f32[256,128]{1,0:T(8,128)} %vec_ref.1, f32[1,256]{1,0:T(1,128)} %bitcast.1), custom_call_target="tpu_custom_call" | custom-call | tf_op jit(solution)/shard_map/pallas_call | solution.py:444
  111.5 1.6 %copy.8 = f32[256,128]{1,0:T(8,128)} copy(f32[256,128]{1,0:T(8,128)} %shard_map.55) | data formatting | bytes 262144

commit v3 on v2

--- a/solution.py
+++ b/solution.py
@@ -38,7 +38,7 @@
     marks_in, marks_unit, kern_t, unit, weighted, stats, side, means,
     side_out, side_in, side_stats_out, side_stats, side_b, shifts,
     image_out, pair_in, line_out, line_in, norms, group_norms,
-    row_sems, stat_sems, grp_sems, img_sems, norm_sems, mark_sems, grown,
+    row_sems, stat_sems, grp_sems, img_sems, norm_sems, mark_sems,
 ):
     own, width = emb_ref.shape
     marks = marks_ref.shape[0]
@@ -249,18 +249,6 @@
 
     lax.fori_loop(0, marks // mark_tile, average, 0)
 
-    def gather_term(step, slot):
-        def visit(i, carry):
-            at = rows_at(i, build_tile)
-            product = nn(
-                kern_t[at, slot * own : (slot + 1) * own],
-                weighted[step, slot * own : (slot + 1) * own, :],
-            )
-            side[at, :] = product if slot == 0 else side[at, :] + product
-            return carry
-
-        lax.fori_loop(0, marks // build_tile, visit, 0)
-
     gaps = None
     mean_row = None
     image = None
@@ -274,7 +262,11 @@
         for j in [*range(1, groups), 0]:
             def centre(i, carry, j=j):
                 at = pl.ds(pl.multiple_of(j * part + i * mark_tile, mark_tile), mark_tile)
-                product = side[at, :] - means[at, 0:1] * totals
+                if step == 0:
+                    product = side[at, :]
+                else:
+                    product = nn(kern_t[at, :], weighted[step])
+                product = product - means[at, 0:1] * totals
                 if j == 0:
                     side[at, :] = product
                 else:
@@ -342,26 +334,16 @@
                 side_b.at[step, 0], side_b.at[step, back],
                 grp_sems.at[step, 3, 1, j], grp_sems.at[step, 3, 0, back], grp=group(j),
             )
-        def term(j, slot):
-            block = kern_t[j * part : (j + 1) * part, slot * own : (slot + 1) * own]
-            return nn(side_b[step, j], block)
-
         for j in range(groups):
             if j:
                 arrived(shifts.at[step, j], grp_sems.at[step, 2, 0, j])
                 shift = shift + shifts[step, j]
                 arrived(side_b.at[step, j], grp_sems.at[step, 3, 0, j])
-            if j < groups - 1:
-                for slot in range(members):
-                    if j == 0:
-                        grown[slot] = term(j, slot)
-                    else:
-                        grown[slot] += term(j, slot)
         shift = jnp.transpose(jnp.broadcast_to(shift[0:1, :], (128, vecs)))[:, 0:1]
 
         def product(slot):
-            last = term(groups - 1, slot) - shift
-            return last if groups == 1 else grown[slot] + last
+            whole = jnp.concatenate([side_b[step, j] for j in range(groups)], axis=1)
+            return nn(whole, kern_t[:, slot * own : (slot + 1) * own]) - shift
 
         for k in [*order, 0]:
             image_out[step, k] = product(line + k).astype(BF16)
@@ -391,16 +373,12 @@
             stats[step + 1, 0, 1:2, 0:vecs] = jnp.sum(full, axis=0, keepdims=True)
             stats[step + 1, 0, 2:3, 0:vecs] = square
             spread_chunk(step + 1)
-            gather_term(step + 1, 0)
-            await_chunk(step + 1, line)
-            gather_term(step + 1, line)
             for k in order:
                 await_chunk(step + 1, line - k)
                 pass_on(step + 1, line - k)
-                gather_term(step + 1, line - k)
+            await_chunk(step + 1, line)
             for k in order:
                 await_chunk(step + 1, 2 * line - k)
-                gather_term(step + 1, 2 * line - k)
 
     norms[0] = jnp.broadcast_to(square, norms.shape[1:])
     for k in range(1, members):
@@ -473,7 +451,6 @@
             dma((ITERS, 2, 2, line)),
             dma((2, members + groups)),
             dma((groups,)),
-            pltpu.VMEM((members, vecs, own), F32),
         ],
         compiler_params=pltpu.CompilerParams(
             collective_id=0, has_side_effects=True, vmem_limit_bytes=62 * 2**20

time: 113 us -> 111 us (0.982)
  Pallas kernels: 111 us -> 108 us
    pallas_call x1, Pallas kernels: 111 us -> 108 us  [local(): pl.pallas_call(functools.partial(kernel, groups, members), out_shape=jax....]
where the time goes in v3:
time: 111 us
  Pallas kernels  108 us (97%)
  local copies, waits for them, and re-layouts  1.57 us (1%)
    pallas_call x1, Pallas kernels, local(): pl.pallas_call(functools.partial(kernel, groups, members), out_shape=jax....  108 us

profile of v3, /device:TPU:0, one launch (start us, length us, event | category | flops | bytes accessed | tf_op | source)
XLA Modules:
  0.0 110.5 jit_solution(2437979209754179243)
XLA Ops:
  0.7 108.3 %shard_map.55 = f32[256,128]{1,0:T(8,128)} custom-call(f32[1]{0:T(128)S(6)} %copy.7.spread_ref, bf16[256,512]{1,0:T(8,128)(2,1)} %emb_ref.1, bf16[2048,512]{1,0:T(8,128)(2,1)} %marks_ref.1, f32[256,128]{1,0:T(8,128)} %vec_ref.1, f32[1,256]{1,0:T(1,128)} %bitcast.1), custom_call_target="tpu_custom_call" | custom-call | tf_op jit(solution)/shard_map/pallas_call | solution.py:422
  109.0 1.6 %copy.8 = f32[256,128]{1,0:T(8,128)} copy(f32[256,128]{1,0:T(8,128)} %shard_map.55) | data formatting | bytes 262144
